TPU v7x, 512 devices: a whole 4x4x16 slice. The times are simulated.
512 devices in a mesh: ep: 64 (over z, y), dp: 8 (over x, core).
Axes of the slice: x: 4, y: 4, z: 16, core: 2. Of those that a mesh axis runs over, the one named last changes fastest.
Arguments:
- tokens: bfloat16 [12288, 3584], P(('ep', 'dp')), may hold values from -6 to 6
- grad_out: bfloat16 [12288, 3584], P(('ep', 'dp')), may hold values from -0.29882812 to 0.29882812
- routes: int32 [12288, 2], P(('ep', 'dp')), may hold values from 0 to 7, all different within a row; in each aligned block of 24 rows (0 to 23, 24 to 47, ...) at most 8 rows name the same one
- route_probs: float32 [12288, 2], P(('ep', 'dp')), may hold values from 0.1 to 1
- gate_weight: bfloat16 [64, 3584, 128], P('ep', 'dp'), may hold values from -0.09375 to 0.09375
- up_weight: bfloat16 [64, 3584, 128], P('ep', 'dp'), may hold values from -0.09375 to 0.09375
- down_weight: bfloat16 [64, 3584, 128], P('ep', 'dp'), may hold values from -0.1875 to 0.1875
Outputs:
- grad_tokens: bfloat16 [12288, 3584], P(('ep', 'dp'))
- grad_probs: float32 [12288, 2], P(('ep', 'dp'))
- grad_gate: bfloat16 [64, 3584, 128], P('ep', 'dp')
- grad_up: bfloat16 [64, 3584, 128], P('ep', 'dp')
- grad_down: bfloat16 [64, 3584, 128], P('ep', 'dp')
Inputs may be any that keep to these rules, and one draw needn't show every extreme that they name: `routes`: each row names 2 different experts. Within each aligned block of 24 rows (the tokens of one device) no expert is named by more than 8 rows; in some blocks one expert is named by exactly 8 rows.
All inputs are finite; a program needn't handle non-finite values.
Results may differ from a plain program's by a relative error of at most 0.017.
Values may be sent and summed in bfloat16 or wider, within the bound.
No kernel may reach another device: no remote copies, remote signals or barrier semaphores. Data moves between devices by JAX's collectives and lax.ppermute only.
A program may use at most 64 MiB of HBM per device.

v0:
```python
import jax
import jax.numpy as jnp
from jax import lax
from jax.sharding import PartitionSpec as P

GROUP = 8
TOP = 2
CONTRACT_HIDDEN = (((1,), (1,)), ((), ()))
CONTRACT_ROWS = (((0,), (0,)), ((), ()))


def slot_layout(routes, experts, capacity):
    flat_routes = routes.reshape(-1)
    copies = flat_routes.shape[0]
    onehot = (flat_routes[:, None] == jnp.arange(experts, dtype=jnp.int32)[None, :]).astype(
        jnp.int32
    )
    earlier = jnp.cumsum(onehot, axis=0) - onehot
    slot_rank = jnp.sum(earlier * onehot, axis=1)
    slot_index = flat_routes * capacity + slot_rank
    slot_copy = jnp.full((experts * capacity,), copies, jnp.int32)
    slot_copy = slot_copy.at[slot_index].set(jnp.arange(copies, dtype=jnp.int32))
    return (slot_index, slot_copy)


def per_device(tokens, grad_out, routes, route_probs, gate_weight, up_weight, down_weight):
    tok_count, features = tokens.shape
    ep_size = lax.axis_size("ep")
    experts = ep_size // GROUP
    slots = min(
        tok_count // GROUP,
        max(1, (4 * TOP * tok_count + 3 * experts * GROUP - 1) // (3 * experts * GROUP)),
    )
    capacity = GROUP * slots
    copies = tok_count * TOP
    slot_index, slot_copy = slot_layout(routes, experts, capacity)
    source_row = jnp.where(slot_copy < copies, slot_copy // TOP, tok_count)
    blank = jnp.zeros((1, features), jnp.bfloat16)
    send_tokens = jnp.concatenate([tokens, blank], axis=0)[source_row]
    send_grads = jnp.concatenate([grad_out, blank], axis=0)[source_row]
    flat_probs = jnp.concatenate([route_probs.reshape(-1), jnp.zeros((1,), jnp.float32)])
    send_probs = flat_probs[slot_copy]
    spread_tokens = jnp.broadcast_to(
        send_tokens.reshape(experts, 1, capacity, features), (experts, GROUP, capacity, features)
    ).reshape(ep_size, capacity, features)
    spread_grads = jnp.broadcast_to(
        send_grads.reshape(experts, 1, capacity, features), (experts, GROUP, capacity, features)
    ).reshape(ep_size, capacity, features)
    spread_probs = jnp.broadcast_to(
        send_probs.reshape(experts, 1, capacity), (experts, GROUP, capacity)
    ).reshape(ep_size, capacity)
    rows_tok, rows_grd, rows_prb = (
        lax.all_to_all(spread_tokens, "ep", split_axis=0, concat_axis=0, tiled=True),
        lax.all_to_all(spread_grads, "ep", split_axis=0, concat_axis=0, tiled=True),
        lax.all_to_all(
            spread_probs.astype(jnp.bfloat16), "ep", split_axis=0, concat_axis=0, tiled=True
        ).astype(spread_probs.dtype),
    )
    rows_in = rows_tok.reshape(-1, features)
    rows_grad = rows_grd.reshape(-1, features)
    rows_prob = rows_prb.reshape(-1)
    gate_all, up_all, down_all = (
        lax.all_gather(gate_weight, "dp", axis=1, tiled=True),
        lax.all_gather(up_weight, "dp", axis=1, tiled=True),
        lax.all_gather(down_weight, "dp", axis=1, tiled=True),
    )
    gate_full = gate_all[0]
    up_full = up_all[0]
    down_full = down_all[0]
    gate_pre = jnp.dot(rows_in, gate_full, preferred_element_type=jnp.float32)
    up_pre = jnp.dot(rows_in, up_full, preferred_element_type=jnp.float32)
    sigmoid_gate = jax.nn.sigmoid(gate_pre)
    activated = gate_pre * sigmoid_gate
    hidden = (activated * up_pre).astype(jnp.bfloat16)
    scaled = (rows_prob[:, None] * rows_grad.astype(jnp.float32)).astype(jnp.bfloat16)
    down_grad = jnp.dot(rows_grad, down_full, preferred_element_type=jnp.float32)
    scores = jnp.sum(hidden.astype(jnp.float32) * down_grad, axis=1)
    hidden_grad = rows_prob[:, None] * down_grad
    gate_grad = (
        hidden_grad * up_pre * sigmoid_gate * (1.0 + gate_pre * (1.0 - sigmoid_gate))
    ).astype(jnp.bfloat16)
    up_grad = (hidden_grad * activated).astype(jnp.bfloat16)
    token_part = (
        lax.dot_general(gate_grad, gate_full, CONTRACT_HIDDEN, preferred_element_type=jnp.float32)
        + lax.dot_general(up_grad, up_full, CONTRACT_HIDDEN, preferred_element_type=jnp.float32)
    ).astype(jnp.bfloat16)
    returned, returned_scores = (
        lax.all_to_all(
            token_part.reshape(ep_size, capacity, features),
            "ep",
            split_axis=0,
            concat_axis=0,
            tiled=True,
        ),
        lax.all_to_all(
            scores.reshape(ep_size, capacity).astype(jnp.bfloat16),
            "ep",
            split_axis=0,
            concat_axis=0,
            tiled=True,
        ).astype(jnp.float32),
    )
    slot_rows = jnp.sum(
        returned.reshape(experts, GROUP, capacity, features), axis=1, dtype=jnp.float32
    ).reshape(experts * capacity, features)
    slot_scores = jnp.sum(returned_scores.reshape(experts, GROUP, capacity), axis=1).reshape(-1)
    gate_term = lax.dot_general(
        rows_in, gate_grad, CONTRACT_ROWS, preferred_element_type=jnp.float32
    )
    up_term = lax.dot_general(rows_in, up_grad, CONTRACT_ROWS, preferred_element_type=jnp.float32)
    down_term = lax.dot_general(scaled, hidden, CONTRACT_ROWS, preferred_element_type=jnp.float32)
    gate_sum, up_sum, down_sum = (
        lax.psum_scatter(
            gate_term.astype(jnp.bfloat16), "dp", scatter_dimension=0, tiled=True
        ).astype(jnp.float32),
        lax.psum_scatter(
            up_term.astype(jnp.bfloat16), "dp", scatter_dimension=0, tiled=True
        ).astype(jnp.float32),
        lax.psum_scatter(
            down_term.astype(jnp.bfloat16), "dp", scatter_dimension=0, tiled=True
        ).astype(jnp.float32),
    )
    grad_tokens = jnp.sum(slot_rows[slot_index].reshape(tok_count, TOP, features), axis=1).astype(
        jnp.bfloat16
    )
    grad_probs = slot_scores[slot_index].reshape(tok_count, TOP)
    grad_gate = gate_sum.astype(jnp.bfloat16)[None]
    grad_up = up_sum.astype(jnp.bfloat16)[None]
    grad_down = down_sum.astype(jnp.bfloat16)[None]
    return (grad_tokens, grad_probs, grad_gate, grad_up, grad_down)


def solution(mesh):
    placed = (
        P(("ep", "dp"), None),
        P(("ep", "dp"), None),
        P(("ep", "dp"), None),
        P(("ep", "dp"), None),
        P("ep", "dp", None),
        P("ep", "dp", None),
        P("ep", "dp", None),
    )
    return jax.shard_map(
        per_device,
        mesh=mesh,
        in_specs=placed,
        out_specs=(
            P(("ep", "dp"), None),
            P(("ep", "dp"), None),
            P("ep", "dp", None),
            P("ep", "dp", None),
            P("ep", "dp", None),
        ),
        check_vma=False,
    )
```

profile of v0, /device:TPU:2, one launch (start us, length us, event | category | flops | bytes accessed | tf_op | source)
XLA Modules:
  0.0 604.3 jit_solution(18068888513377550808)
XLA Ops:
  7.2 0.7 broadcast_multiply_fusion
  7.8 0.8 copy.27
  8.6 0.8 copy.25
  9.4 0.1 reshape.119
  9.5 0.1 copy.26
  9.6 0.1 mul.61
  9.7 0.1 eq.15
  9.8 0.1 fusion.18
  9.8 0.1 reduce_window_sum.11
  9.9 0.2 select_reduce_fusion
  10.1 0.7 scatter_custom_fusion
  10.9 0.1 pad_maximum_fusion
  11.0 0.8 gather_fusion
  11.7 0.1 convert_element_type.101
  11.8 0.1 copy.28
  11.9 0.1 broadcast_in_dim.45
  12.0 0.1 convert_element_type.102
  12.1 0.7 copy.29
  12.8 18.7 %all-to-all-start = ((bf16[64,1,8]{2,1,0:T(2,128)(2,1)}), bf16[64,1,8]{2,1,0:T(2,128)(2,1)S(1)}, u32[]{:S(2)}, u32[]{:S(2)}) async-start(bf16[64,1,8]{2,1,0:T(2,128)(2,1)} %copy.29), calls=%async_computation | async-start | bytes 65536 | tf_op jit(solution)/shard_map/all_to_all | solution.py:55
  31.6 0.9 concatenate.11
  32.5 0.8 gather_fusion.2
  33.3 12.8 %all-to-all-done = bf16[64,1,8]{2,1,0:T(2,128)(2,1)S(1)} async-done(((bf16[64,1,8]{2,1,0:T(2,128)(2,1)}), bf16[64,1,8]{2,1,0:T(2,128)(2,1)S(1)}, u32[]{:S(2)}, u32[]{:S(2)}) %all-to-all-start) | async-done | bytes 1056 | tf_op jit(solution)/shard_map/all_to_all | solution.py:55
  46.1 2.1 broadcast_in_dim.51
  48.2 5.7 all-to-all-start.2
  53.9 0.0 copy-done
  54.0 0.8 gather_fusion.1
  54.8 165.5 %all-to-all-done.2 = bf16[64,8,3584]{2,1,0:T(8,128)(2,1)} async-done(((bf16[64,8,3584]{2,1,0:T(8,128)(2,1)}), bf16[64,8,3584]{2,1,0:T(8,128)(2,1)}, u32[]{:S(2)}, u32[]{:S(2)}) %all-to-all-start.2) | async-done | bytes 3670048 | tf_op jit(solution)/shard_map/all_to_all | solution.py:53
  220.3 2.1 broadcast_in_dim.49
  222.4 6.2 %all-to-all-start.1 = ((bf16[64,8,3584]{2,1,0:T(8,128)(2,1)}), bf16[64,8,3584]{2,1,0:T(8,128)(2,1)}, u32[]{:S(2)}, u32[]{:S(2)}) async-start(bf16[64,8,3584]{2,1,0:T(8,128)(2,1)} %bitcast.64), calls=%async_computation.1 | async-start | bytes 7340032 | tf_op jit(solution)/shard_map/all_to_all | solution.py:54
  228.6 0.0 copy-done.1
  228.6 13.6 %all_gather.11 = bf16[1,3584,128]{2,1,0:T(8,128)(2,1)S(1)} all-gather(bf16[1,448,128]{2,1,0:T(8,128)(2,1)S(1)} %copy-done.1), channel_id=1, replica_groups=mesh['ep'=64,'dp'=8] {'dp'}, dimensions={1}, use_global_device_ids=true | all-gather | bytes 1032192 | tf_op jit(solution)/shard_map/all_gather | solution.py:63
  242.3 13.5 %all_gather.10 = bf16[1,3584,128]{2,1,0:T(8,128)(2,1)S(1)} all-gather(bf16[1,448,128]{2,1,0:T(8,128)(2,1)S(1)} %copy-done.2), channel_id=1, replica_groups=mesh['ep'=64,'dp'=8] {'dp'}, dimensions={1}, use_global_device_ids=true | all-gather | bytes 1032192 | tf_op jit(solution)/shard_map/all_gather | solution.py:64
  255.8 13.5 %all_gather.9 = bf16[1,3584,128]{2,1,0:T(8,128)(2,1)S(1)} all-gather(bf16[1,448,128]{2,1,0:T(8,128)(2,1)S(1)} %copy-done.3), channel_id=1, replica_groups=mesh['ep'=64,'dp'=8] {'dp'}, dimensions={1}, use_global_device_ids=true | all-gather | bytes 1032192 | tf_op jit(solution)/shard_map/all_gather | solution.py:65
  269.3 0.1 convert_reduce_fusion.1
  269.4 0.1 reshape.129
  269.4 3.4 fusion.3
  272.8 3.4 fusion.5
  276.2 119.3 %all-to-all-done.1 = bf16[64,8,3584]{2,1,0:T(8,128)(2,1)} async-done(((bf16[64,8,3584]{2,1,0:T(8,128)(2,1)}), bf16[64,8,3584]{2,1,0:T(8,128)(2,1)}, u32[]{:S(2)}, u32[]{:S(2)}) %all-to-all-start.1) | async-done | bytes 3670048 | tf_op jit(solution)/shard_map/all_to_all | solution.py:54
  395.5 4.1 multiply_reduce_fusion
  399.6 0.7 convert_element_type.125
  400.3 6.0 all-to-all-start.4
  406.4 1.1 fusion.11
  407.5 3.1 fusion
  410.6 10.2 %all-to-all-done.4 = bf16[64,1,8]{2,1,0:T(2,128)(2,1)S(1)} async-done(((bf16[64,1,8]{2,1,0:T(2,128)(2,1)}), bf16[64,1,8]{2,1,0:T(2,128)(2,1)S(1)}, u32[]{:S(2)}, u32[]{:S(2)}) %all-to-all-start.4) | async-done | bytes 1056 | tf_op jit(solution)/shard_map/all_to_all | solution.py:95
  420.8 5.6 all-to-all-start.3
  426.4 0.0 reduce-scatter.8.cloned.1.call-start
  426.4 0.0 copy-done.4
  426.5 4.4 convolution_convert_fusion
  430.8 0.0 reduce-scatter.8.cloned.1.call-update
  430.9 0.0 reduce-scatter.6.cloned.1.call-start
  430.9 4.1 convolution_convert_fusion.1
  435.1 0.0 reduce-scatter.6.cloned.1.call-update
  435.1 0.0 reduce-scatter.4.cloned.1.call-start
  435.1 4.1 convolution_convert_fusion.2
  439.3 0.0 reduce-scatter.4.cloned.1.call-update
  439.4 0.1 reshape.127
  439.5 0.8 gather_fusion.4
  440.2 0.1 reshape.128
  440.3 0.6 copy.31
  441.0 151.4 %all-to-all-done.3 = bf16[64,8,3584]{2,1,0:T(8,128)(2,1)} async-done(((bf16[64,8,3584]{2,1,0:T(8,128)(2,1)}), bf16[64,8,3584]{2,1,0:T(8,128)(2,1)}, u32[]{:S(2)}, u32[]{:S(2)}) %all-to-all-start.3) | async-done | bytes 3670048 | tf_op jit(solution)/shard_map/all_to_all | solution.py:88
  592.4 2.6 convert_reduce_fusion
  595.0 0.8 gather_fusion.3
  595.8 0.4 reshape.126
  596.2 1.5 reduce_sum.50
  (18 shorter events, 0.1 us)
Async XLA Ops:
  12.8 33.3 %all-to-all-start = ((bf16[64,1,8]{2,1,0:T(2,128)(2,1)}), bf16[64,1,8]{2,1,0:T(2,128)(2,1)S(1)}, u32[]{:S(2)}, u32[]{:S(2)}) async-start(bf16[64,1,8]{2,1,0:T(2,128)(2,1)} %copy.29), calls=%async_computation | async-start | bytes 65536 | tf_op jit(solution)/shard_map/all_to_all | solution.py:55
  48.2 5.8 copy-start
  48.2 172.1 %all-to-all-start.2 = ((bf16[64,8,3584]{2,1,0:T(8,128)(2,1)}), bf16[64,8,3584]{2,1,0:T(8,128)(2,1)}, u32[]{:S(2)}, u32[]{:S(2)}) async-start(bf16[64,8,3584]{2,1,0:T(8,128)(2,1)} %bitcast.65), calls=%async_computation.2 | async-start | bytes 7340032 | tf_op jit(solution)/shard_map/all_to_all | solution.py:53
  222.4 6.2 %copy-start.1 = (bf16[1,448,128]{2,1,0:T(8,128)(2,1)S(1)}, bf16[1,448,128]{2,1,0:T(8,128)(2,1)}, u32[]{:S(2)}) copy-start(bf16[1,448,128]{2,1,0:T(8,128)(2,1)} %param.11) | copy-start | bytes 344068
  222.4 19.8 %copy-start.2 = (bf16[1,448,128]{2,1,0:T(8,128)(2,1)S(1)}, bf16[1,448,128]{2,1,0:T(8,128)(2,1)}, u32[]{:S(2)}) copy-start(bf16[1,448,128]{2,1,0:T(8,128)(2,1)} %param.12) | copy-start | bytes 344068
  222.4 33.3 %copy-start.3 = (bf16[1,448,128]{2,1,0:T(8,128)(2,1)S(1)}, bf16[1,448,128]{2,1,0:T(8,128)(2,1)}, u32[]{:S(2)}) copy-start(bf16[1,448,128]{2,1,0:T(8,128)(2,1)} %param.13) | copy-start | bytes 344068
  222.4 173.1 %all-to-all-start.1 = ((bf16[64,8,3584]{2,1,0:T(8,128)(2,1)}), bf16[64,8,3584]{2,1,0:T(8,128)(2,1)}, u32[]{:S(2)}, u32[]{:S(2)}) async-start(bf16[64,8,3584]{2,1,0:T(8,128)(2,1)} %bitcast.64), calls=%async_computation.1 | async-start | bytes 7340032 | tf_op jit(solution)/shard_map/all_to_all | solution.py:54
  400.3 20.4 %all-to-all-start.4 = ((bf16[64,1,8]{2,1,0:T(2,128)(2,1)}), bf16[64,1,8]{2,1,0:T(2,128)(2,1)S(1)}, u32[]{:S(2)}, u32[]{:S(2)}) async-start(bf16[64,1,8]{2,1,0:T(2,128)(2,1)} %convert_element_type.125), calls=%async_computation.4 | async-start | bytes 65536 | tf_op jit(solution)/shard_map/all_to_all | solution.py:95
  410.6 15.9 %copy-start.4 = (bf16[512,128]{0,1:T(8,128)(2,1)S(1)}, bf16[512,128]{0,1:T(8,128)(2,1)}, u32[]{:S(2)}) copy-start(bf16[512,128]{0,1:T(8,128)(2,1)} %get-tuple-element.26) | copy-start | bytes 393220
  420.8 171.6 %all-to-all-start.3 = ((bf16[64,8,3584]{2,1,0:T(8,128)(2,1)}), bf16[64,8,3584]{2,1,0:T(8,128)(2,1)}, u32[]{:S(2)}, u32[]{:S(2)}) async-start(bf16[64,8,3584]{2,1,0:T(8,128)(2,1)} %fusion), calls=%async_computation.3 | async-start | bytes 7340032 | tf_op jit(solution)/shard_map/all_to_all | solution.py:88
  426.4 171.3 %reduce-scatter.8.cloned.1.call-start = ((), (), s32[]{:S(2)}) async-start(), calls=%async_computation.10 | async-start | bytes 1032192 | tf_op jit(solution)/shard_map/reduce_scatter | solution.py:119
  430.9 166.9 %reduce-scatter.6.cloned.1.call-start = ((), (), s32[]{:S(2)}) async-start(), calls=%async_computation.9 | async-start | bytes 1032192 | tf_op jit(solution)/shard_map/reduce_scatter | solution.py:116
  435.1 162.7 %reduce-scatter.4.cloned.1.call-start = ((), (), s32[]{:S(2)}) async-start(), calls=%async_computation.8 | async-start | bytes 1032192 | tf_op jit(solution)/shard_map/reduce_scatter | solution.py:113
Sparse Core Ops, SparseCore 0:
  431.0 37.9 reduce-scatter.7
  472.3 39.6 reduce-scatter.5
  515.5 39.6 reduce-scatter.3
where the time goes:
time: 605 us; the launch traced here: 604 us
  waiting for transfers between devices  459 us (76%)
  starting transfers between devices  42.4 us (7%)
  blocking collectives  40.6 us (7%)
  matrix products  27.7 us (5%)
  local copies, waits for them, and re-layouts  14.9 us (2%)
  between operations  14 us (2%)
    all_to_all x1, waiting for transfers between devices, per_device(): lax.all_to_all(spread_tokens, 'ep', split_axis=0, concat_axis=0, tiled=True)  166 us
    all_to_all x1, waiting for transfers between devices, per_device(): lax.all_to_all(token_part.reshape(ep_size, capacity, features), 'ep', spl...  151 us
    all_to_all x1, waiting for transfers between devices, per_device(): lax.all_to_all(spread_grads, 'ep', split_axis=0, concat_axis=0, tiled=True)  119 us
    all_to_all x1, starting transfers between devices, per_device(): lax.all_to_all(spread_probs.astype(jnp.bfloat16), 'ep', split_axis=0, con...  18.7 us
    all_gather x1, blocking collectives, per_device(): lax.all_gather(gate_weight, 'dp', axis=1, tiled=True)  13.6 us
    all_gather x1, blocking collectives, per_device(): lax.all_gather(up_weight, 'dp', axis=1, tiled=True)  13.5 us
    all_gather x1, blocking collectives, per_device(): lax.all_gather(down_weight, 'dp', axis=1, tiled=True)  13.5 us
    all_to_all x1, waiting for transfers between devices, per_device(): lax.all_to_all(spread_probs.astype(jnp.bfloat16), 'ep', split_axis=0, con...  12.8 us
  transfers between devices with their start and end apart: 8, of which 5 were waited for; matrix products, arithmetic and copies ran while one was open for 6% of the time, Pallas kernels for 0%

commit v1 on v0

--- a/solution.py
+++ b/solution.py
@@ -61,7 +61,9 @@
     rows_prob = rows_prb.reshape(-1)
     gate_all, up_all, down_all = (
         lax.all_gather(gate_weight, "dp", axis=1, tiled=True),
-        lax.all_gather(up_weight, "dp", axis=1, tiled=True),
+        jnp.concatenate(
+            lax.all_to_all(jnp.stack([up_weight] * lax.axis_size("dp")), "dp", 0, 0), axis=1
+        ),
         lax.all_gather(down_weight, "dp", axis=1, tiled=True),
     )
     gate_full = gate_all[0]

time: 605 us -> 626 us (1.035)
  the two profiles are of different devices: /device:TPU:2 before, /device:TPU:8 now
where the time goes in v1:
time: 626 us
  waiting for transfers between devices  474 us (76%)
  blocking collectives  59.5 us (10%)
  starting transfers between devices  29.3 us (5%)
  matrix products  27.8 us (4%)
  local copies, waits for them, and re-layouts  15.4 us (2%)
  between operations  14 us (2%)
    all_to_all x1, waiting for transfers between devices, per_device(): lax.all_to_all(spread_tokens, 'ep', split_axis=0, concat_axis=0, tiled=True)  167 us
    all_to_all x1, waiting for transfers between devices, per_device(): lax.all_to_all(token_part.reshape(ep_size, capacity, features), 'ep', spl...  151 us
    all_to_all x1, waiting for transfers between devices, per_device(): lax.all_to_all(spread_grads, 'ep', split_axis=0, concat_axis=0, tiled=True)  133 us
    all_to_all x1, blocking collectives, per_device(): lax.all_to_all(spread_probs.astype(jnp.bfloat16), 'ep', split_axis=0, con...  32.3 us
    all_to_all x1, waiting for transfers between devices, per_device(): lax.all_to_all(jnp.stack([up_weight] * lax.axis_size('dp')), 'dp', 0, 0)  13.7 us
    all_gather x1, blocking collectives, per_device(): lax.all_gather(gate_weight, 'dp', axis=1, tiled=True)  13.6 us
    all_gather x1, blocking collectives, per_device(): lax.all_gather(down_weight, 'dp', axis=1, tiled=True)  13.5 us
  transfers between devices with their start and end apart: 8, of which 5 were waited for; matrix products, arithmetic and copies ran while one was open for 5% of the time, Pallas kernels for 0%

profile of v1, /device:TPU:8, one launch (start us, length us, event | category | flops | bytes accessed | tf_op | source)
XLA Modules:
  0.0 625.6 jit_solution(13486019773526643766)
XLA Ops:
  7.2 0.0 copy-start.1
  7.2 0.7 broadcast_multiply_fusion
  7.9 0.8 copy.27
  8.7 0.8 copy.25
  9.4 0.1 reshape.122
  9.5 0.1 copy.26
  9.6 0.1 mul.61
  9.7 0.1 eq.15
  9.8 0.1 fusion.16
  9.9 0.1 reduce_window_sum.11
  10.0 0.2 select_reduce_fusion
  10.2 0.7 scatter_custom_fusion
  10.9 0.1 pad_maximum_fusion
  11.0 0.8 gather_fusion
  11.8 0.1 convert_element_type.101
  11.9 0.1 copy.28
  12.0 0.1 broadcast_in_dim.45
  12.0 0.1 convert_element_type.102
  12.1 0.1 copy.29
  12.2 32.3 %all_to_all.32 = bf16[64,1,8]{2,1,0:T(2,128)(2,1)S(1)} all-to-all(bf16[64,1,8]{2,1,0:T(2,128)(2,1)S(1)} %copy.29), channel_id=1, replica_groups=mesh['ep'=64,'dp'=8] {'ep'}, dimensions={0} | all-to-all | bytes 2048 | tf_op jit(solution)/shard_map/all_to_all | solution.py:55
  44.6 1.9 stack.2
  46.5 4.3 all-to-all-start.3
  50.8 0.0 copy-done.1
  50.9 0.8 gather_fusion.2
  51.7 13.7 %all-to-all-done.3 = bf16[8,1,448,128]{3,2,1,0:T(8,128)(2,1)S(1)} async-done(((bf16[8,1,448,128]{3,2,1,0:T(8,128)(2,1)}), bf16[8,1,448,128]{3,2,1,0:T(8,128)(2,1)S(1)}, u32[]{:S(2)}, u32[]{:S(2)}) %all-to-all-start.3) | async-done | bytes 917536 | tf_op jit(solution)/shard_map/all_to_all | solution.py:65
  65.4 2.1 broadcast_in_dim.51
  67.5 6.4 %all-to-all-start.2 = ((bf16[64,8,3584]{2,1,0:T(8,128)(2,1)}), bf16[64,8,3584]{2,1,0:T(8,128)(2,1)}, u32[]{:S(2)}, u32[]{:S(2)}) async-start(bf16[64,8,3584]{2,1,0:T(8,128)(2,1)} %bitcast.64), calls=%async_computation.2 | async-start | bytes 7340032 | tf_op jit(solution)/shard_map/all_to_all | solution.py:53
  73.8 0.0 copy-done.2
  73.9 0.8 gather_fusion.1
  74.7 166.7 %all-to-all-done.2 = bf16[64,8,3584]{2,1,0:T(8,128)(2,1)} async-done(((bf16[64,8,3584]{2,1,0:T(8,128)(2,1)}), bf16[64,8,3584]{2,1,0:T(8,128)(2,1)}, u32[]{:S(2)}, u32[]{:S(2)}) %all-to-all-start.2) | async-done | bytes 3670048 | tf_op jit(solution)/shard_map/all_to_all | solution.py:53
  241.4 2.2 broadcast_in_dim.49
  243.6 6.2 all-to-all-start.1
  249.8 13.6 %all_gather.7 = bf16[1,3584,128]{2,1,0:T(8,128)(2,1)S(1)} all-gather(bf16[1,448,128]{2,1,0:T(8,128)(2,1)S(1)} %copy-done.3), channel_id=1, replica_groups=mesh['ep'=64,'dp'=8] {'dp'}, dimensions={1}, use_global_device_ids=true | all-gather | bytes 1032192 | tf_op jit(solution)/shard_map/all_gather | solution.py:63
  263.5 13.5 %all_gather.6 = bf16[1,3584,128]{2,1,0:T(8,128)(2,1)S(1)} all-gather(bf16[1,448,128]{2,1,0:T(8,128)(2,1)S(1)} %copy-done.4), channel_id=1, replica_groups=mesh['ep'=64,'dp'=8] {'dp'}, dimensions={1}, use_global_device_ids=true | all-gather | bytes 1032192 | tf_op jit(solution)/shard_map/all_gather | solution.py:67
  277.0 0.1 convert_reduce_fusion.1
  277.1 0.1 reshape.132
  277.2 3.4 fusion.3
  280.5 3.4 fusion.5
  283.9 132.8 %all-to-all-done.1 = bf16[64,8,3584]{2,1,0:T(8,128)(2,1)} async-done(((bf16[64,8,3584]{2,1,0:T(8,128)(2,1)}), bf16[64,8,3584]{2,1,0:T(8,128)(2,1)}, u32[]{:S(2)}, u32[]{:S(2)}) %all-to-all-start.1) | async-done | bytes 3670048 | tf_op jit(solution)/shard_map/all_to_all | solution.py:54
  416.8 4.1 multiply_reduce_fusion
  420.9 0.7 convert_element_type.125
  421.6 6.0 all-to-all-start.5
  427.6 1.1 fusion.11
  428.8 3.1 fusion
  431.9 9.5 %all-to-all-done.5 = bf16[64,1,8]{2,1,0:T(2,128)(2,1)S(1)} async-done(((bf16[64,1,8]{2,1,0:T(2,128)(2,1)}), bf16[64,1,8]{2,1,0:T(2,128)(2,1)S(1)}, u32[]{:S(2)}, u32[]{:S(2)}) %all-to-all-start.5) | async-done | bytes 1056 | tf_op jit(solution)/shard_map/all_to_all | solution.py:97
  441.3 6.3 %all-to-all-start.4 = ((bf16[64,8,3584]{2,1,0:T(8,128)(2,1)}), bf16[64,8,3584]{2,1,0:T(8,128)(2,1)}, u32[]{:S(2)}, u32[]{:S(2)}) async-start(bf16[64,8,3584]{2,1,0:T(8,128)(2,1)} %fusion), calls=%async_computation.4 | async-start | bytes 7340032 | tf_op jit(solution)/shard_map/all_to_all | solution.py:90
  447.6 0.0 reduce-scatter.8.cloned.1.call-start
  447.7 4.4 convolution_convert_fusion
  452.1 0.0 reduce-scatter.8.cloned.1.call-update
  452.1 0.0 reduce-scatter.6.cloned.1.call-start
  452.1 4.1 convolution_convert_fusion.1
  456.3 0.0 reduce-scatter.6.cloned.1.call-update
  456.3 0.0 reduce-scatter.4.cloned.1.call-start
  456.3 4.1 convolution_convert_fusion.2
  460.5 0.0 reduce-scatter.4.cloned.1.call-update
  460.6 0.1 reshape.130
  460.7 0.8 gather_fusion.4
  461.4 0.1 reshape.131
  461.5 0.6 copy.31
  462.2 151.5 %all-to-all-done.4 = bf16[64,8,3584]{2,1,0:T(8,128)(2,1)} async-done(((bf16[64,8,3584]{2,1,0:T(8,128)(2,1)}), bf16[64,8,3584]{2,1,0:T(8,128)(2,1)}, u32[]{:S(2)}, u32[]{:S(2)}) %all-to-all-start.4) | async-done | bytes 3670048 | tf_op jit(solution)/shard_map/all_to_all | solution.py:90
  613.7 2.6 convert_reduce_fusion
  616.3 0.8 gather_fusion.3
  617.1 0.4 reshape.129
  617.5 1.5 reduce_sum.50
  (21 shorter events, 0.1 us)
Async XLA Ops:
  7.2 43.7 %copy-start.1 = (bf16[24,3584]{1,0:T(8,128)(2,1)S(1)}, bf16[24,3584]{1,0:T(8,128)(2,1)}, u32[]{:S(2)}) copy-start(bf16[24,3584]{1,0:T(8,128)(2,1)} %param.7) | copy-start | bytes 516100
  46.5 18.8 %all-to-all-start.3 = ((bf16[8,1,448,128]{3,2,1,0:T(8,128)(2,1)}), bf16[8,1,448,128]{3,2,1,0:T(8,128)(2,1)S(1)}, u32[]{:S(2)}, u32[]{:S(2)}) async-start(bf16[8,1,448,128]{3,2,1,0:T(8,128)(2,1)} %stack.2), calls=%async_computation.3 | async-start | bytes 1835008 | tf_op jit(solution)/shard_map/all_to_all | solution.py:65
  67.5 6.4 %copy-start.2 = (bf16[24,3584]{1,0:T(8,128)(2,1)S(1)}, bf16[24,3584]{1,0:T(8,128)(2,1)}, u32[]{:S(2)}) copy-start(bf16[24,3584]{1,0:T(8,128)(2,1)} %param.8) | copy-start | bytes 516100
  67.5 174.0 %all-to-all-start.2 = ((bf16[64,8,3584]{2,1,0:T(8,128)(2,1)}), bf16[64,8,3584]{2,1,0:T(8,128)(2,1)}, u32[]{:S(2)}, u32[]{:S(2)}) async-start(bf16[64,8,3584]{2,1,0:T(8,128)(2,1)} %bitcast.64), calls=%async_computation.2 | async-start | bytes 7340032 | tf_op jit(solution)/shard_map/all_to_all | solution.py:53
  243.6 6.3 %copy-start.3 = (bf16[1,448,128]{2,1,0:T(8,128)(2,1)S(1)}, bf16[1,448,128]{2,1,0:T(8,128)(2,1)}, u32[]{:S(2)}) copy-start(bf16[1,448,128]{2,1,0:T(8,128)(2,1)} %param.11) | copy-start | bytes 344068
  243.6 19.9 %copy-start.4 = (bf16[1,448,128]{2,1,0:T(8,128)(2,1)S(1)}, bf16[1,448,128]{2,1,0:T(8,128)(2,1)}, u32[]{:S(2)}) copy-start(bf16[1,448,128]{2,1,0:T(8,128)(2,1)} %param.13) | copy-start | bytes 344068
  243.6 173.2 %all-to-all-start.1 = ((bf16[64,8,3584]{2,1,0:T(8,128)(2,1)}), bf16[64,8,3584]{2,1,0:T(8,128)(2,1)}, u32[]{:S(2)}, u32[]{:S(2)}) async-start(bf16[64,8,3584]{2,1,0:T(8,128)(2,1)} %bitcast.63), calls=%async_computation.1 | async-start | bytes 7340032 | tf_op jit(solution)/shard_map/all_to_all | solution.py:54
  421.6 19.7 %all-to-all-start.5 = ((bf16[64,1,8]{2,1,0:T(2,128)(2,1)}), bf16[64,1,8]{2,1,0:T(2,128)(2,1)S(1)}, u32[]{:S(2)}, u32[]{:S(2)}) async-start(bf16[64,1,8]{2,1,0:T(2,128)(2,1)} %convert_element_type.125), calls=%async_computation.5 | async-start | bytes 65536 | tf_op jit(solution)/shard_map/all_to_all | solution.py:97
  427.6 1.2 copy-start
  431.9 15.8 %copy-start.5 = (bf16[512,128]{0,1:T(8,128)(2,1)S(1)}, bf16[512,128]{0,1:T(8,128)(2,1)}, u32[]{:S(2)}) copy-start(bf16[512,128]{0,1:T(8,128)(2,1)} %get-tuple-element.26) | copy-start | bytes 393220
  441.3 172.3 %all-to-all-start.4 = ((bf16[64,8,3584]{2,1,0:T(8,128)(2,1)}), bf16[64,8,3584]{2,1,0:T(8,128)(2,1)}, u32[]{:S(2)}, u32[]{:S(2)}) async-start(bf16[64,8,3584]{2,1,0:T(8,128)(2,1)} %fusion), calls=%async_computation.4 | async-start | bytes 7340032 | tf_op jit(solution)/shard_map/all_to_all | solution.py:90
  447.6 171.4 %reduce-scatter.8.cloned.1.call-start = ((), (), s32[]{:S(2)}) async-start(), calls=%async_computation.11 | async-start | bytes 1032192 | tf_op jit(solution)/shard_map/reduce_scatter | solution.py:121
  452.1 167.0 %reduce-scatter.6.cloned.1.call-start = ((), (), s32[]{:S(2)}) async-start(), calls=%async_computation.10 | async-start | bytes 1032192 | tf_op jit(solution)/shard_map/reduce_scatter | solution.py:118
  456.3 162.7 %reduce-scatter.4.cloned.1.call-start = ((), (), s32[]{:S(2)}) async-start(), calls=%async_computation.9 | async-start | bytes 1032192 | tf_op jit(solution)/shard_map/reduce_scatter | solution.py:115
Sparse Core Ops, SparseCore 0:
  452.2 39.4 reduce-scatter.7
  495.1 39.5 reduce-scatter.5
  538.1 39.6 reduce-scatter.3
